TPU v7x, 32 devices: a whole 2x2x4 slice. The times are simulated.
32 devices in a mesh: term: 8 (over z, x), sector: 4 (over y, core).
Axes of the slice: x: 2, y: 2, z: 4, core: 2. Of those that a mesh axis runs over, the one named last changes fastest.
Arguments:
- psi_start: float32 [4, 384, 384], P('sector'), may hold values from -6 to 6
- diagonal: float32 [4, 384, 384], P('sector'), may hold values from -3 to 3
- left_ops: float32 [128, 384, 384], P(('term', 'sector')), may hold values from -0.3125 to 0.3125
- right_ops: float32 [128, 384, 384], P(('term', 'sector')), may hold values from -0.078125 to 0.078125
- pair_in: int32 [32, 4], P(('term', 'sector')), may hold values from 0 to 3
- pair_out: int32 [32, 4], P(('term', 'sector')), may hold values from 0 to 3
- pair_count: int32 [32], P(('term', 'sector')), may hold values from 1 to 4, as said below
Outputs:
- psi_final: float32 [4, 384, 384], P('sector')
- energies: float32 [2], replicated
Inputs may be any that keep to these rules, and one draw needn't show every extreme that they name: `pair_count`: some device has all 4 slots live in every draw.
All inputs are finite; a program needn't handle non-finite values.
Results may differ from a plain program's by a relative error of at most 0.00013.
Values sent between devices are 32-bit elements; how exact they have to be, the bound alone decides.
No kernel may reach another device: no remote copies, remote signals or barrier semaphores. Data moves between devices by JAX's collectives and lax.ppermute only.
A program may use at most 64 MiB of HBM per device.

v0:
```python
import jax
import jax.numpy as jnp
from jax import lax
from jax.sharding import PartitionSpec as P

ITERS = 2
epsilon = 1e-06


def apply_pairs(gathered, left_ops, right_ops, pair_in, pair_out, pair_count):

    def one_pair(pair_slot, partial_value):
        source = lax.dynamic_index_in_dim(gathered, pair_in[0, pair_slot], 0, keepdims=False)
        left_block = lax.dynamic_index_in_dim(left_ops, pair_slot, 0, keepdims=False)
        right_block = lax.dynamic_index_in_dim(right_ops, pair_slot, 0, keepdims=False)
        inner_prod = jnp.dot(left_block, source, precision=lax.Precision.HIGHEST)
        product = lax.dot_general(
            inner_prod, right_block, (((1,), (1,)), ((), ())), precision=lax.Precision.HIGHEST
        )
        target = pair_out[0, pair_slot]
        current = lax.dynamic_index_in_dim(partial_value, target, 0, keepdims=False)
        return lax.dynamic_update_index_in_dim(partial_value, current + product, target, 0)

    return lax.fori_loop(0, pair_count[0], one_pair, jnp.zeros(gathered.shape, jnp.float32))


def global_sums(values):
    return lax.psum((values[0],), "sector")


def sigma_blocks(vector, left_ops, right_ops, pair_in, pair_out, pair_count):
    gathered = lax.all_gather(vector, "sector", axis=0, tiled=True)
    partial_value = apply_pairs(gathered, left_ops, right_ops, pair_in, pair_out, pair_count)
    owned_sum = lax.psum_scatter(partial_value, "sector", scatter_dimension=0, tiled=True)
    return lax.psum(owned_sum, "term")


def shards(psi_start, diagonal, left_ops, right_ops, pair_in, pair_out, pair_count):
    vector = psi_start
    cell_total = float(
        psi_start.shape[0] * lax.axis_size("sector") * psi_start.shape[1] * psi_start.shape[2]
    )
    energies = []
    for sweep in range(ITERS):
        vec_share = vector
        squares = global_sums((jnp.sum(vec_share * vec_share),))[0]
        inverse_norm = 1.0 / jnp.sqrt(squares / cell_total + epsilon)
        normed = vector * inverse_norm
        sigma = sigma_blocks(normed, left_ops, right_ops, pair_in, pair_out, pair_count)
        product_sum = global_sums((jnp.sum(normed * sigma),))[0]
        rayleigh = product_sum / cell_total
        residual = sigma - rayleigh * normed
        correction = residual / jnp.maximum(jnp.abs(diagonal - rayleigh), 1.0)
        updated = normed - correction
        vector = updated
        energies.append(rayleigh)
    return (vector, jnp.stack(energies))


def solution(mesh):
    return jax.shard_map(
        shards,
        mesh=mesh,
        in_specs=(
            P("sector", None, None),
            P("sector", None, None),
            P(("term", "sector"), None, None),
            P(("term", "sector"), None, None),
            P(("term", "sector"), None),
            P(("term", "sector"), None),
            P(("term", "sector")),
        ),
        out_specs=(P("sector", None, None), P()),
        check_vma=False,
    )
```

profile of v0, /device:TPU:0, one launch (start us, length us, event | category | flops | bytes accessed | tf_op | source)
XLA Modules:
  0.0 407.2 jit_solution(11676332899711747829)
XLA Ops:
  7.2 0.0 copy-start.4
  7.2 0.0 copy-start.5
  7.2 0.0 all-gather.3.cloned.1.call-start
  7.2 1.8 multiply_reduce_fusion.3
  9.1 9.0 %psum.42 = f32[]{:T(128)} all-reduce(f32[]{:T(128)} %multiply_reduce_fusion.3), channel_id=1, replica_groups=mesh['term'=8,'sector'=4] {'sector'}, use_global_device_ids=true, to_apply=%region_1.0 | all-reduce | flops 1 | bytes 8 | tf_op jit(solution)/shard_map/psum | solution.py:28
  18.7 1.9 broadcast_multiply_fusion.1
  20.7 0.0 all-gather.3.cloned.1.call-update
  20.7 0.0 reduce-scatter.3.cloned.1.call-start
  20.7 24.4 %all-gather.3.cloned.1.call-done = f32[4,384,384]{2,1,0:T(8,128)} async-done(((f32[1,384,384]{2,1,0:T(8,128)}), f32[4,384,384]{2,1,0:T(8,128)}) %all-gather.3.cloned.1.call-update) | async-done | bytes 2359312 | tf_op jit(solution)/shard_map/all_gather | solution.py:32
  45.2 0.2 broadcast.6.clone
  45.4 39.8 %while.20 = (s32[]{:T(128)}, f32[4,384,384]{2,1,0:T(8,128)S(1)}, s32[]{:T(128)}, s32[1,4]{1,0:T(1,128)S(1)}, f32[4,384,384]{2,1,0:T(8,128)}, /*index=5*/s32[1,4]...) while((s32[]{:T(128)}, f32[4,384,384]{2,1,0:T(8,128)S(1)}, ...), condition=%wide.region_3.4_spmd, body=%wide.region_2.3_spmd.sunk | while | flops 1359101952 | bytes 5308675 | solution.py:24
  46.0 0.6 constant_dynamic-slice_fusion.10
  50.2 2.5 fusion.40
  52.8 2.3 fusion.41
  55.8 0.6 constant_dynamic-slice_fusion.10
  60.0 2.5 fusion.40
  62.6 2.3 fusion.41
  65.6 0.6 constant_dynamic-slice_fusion.10
  69.8 2.5 fusion.40
  72.4 2.3 fusion.41
  75.4 0.6 constant_dynamic-slice_fusion.10
  79.6 2.5 fusion.40
  82.1 2.3 fusion.41
  85.1 0.0 copy-start.2
  85.2 0.0 copy-start.3
  85.2 1.4 copy-done.1
  86.5 0.0 reduce-scatter.3.cloned.1.call-update
  86.6 0.0 all-reduce.3.cloned.1.call-start
  86.6 32.9 %reduce-scatter.3.cloned.1.call-done = f32[1,384,384]{2,1,0:T(8,128)} async-done(((f32[4,384,384]{2,1,0:T(8,128)}), f32[1,384,384]{2,1,0:T(8,128)}) %reduce-scatter.3.cloned.1.call-update) | async-done | bytes 589840 | tf_op jit(solution)/shard_map/reduce_scatter | solution.py:34
  119.5 0.0 all-reduce.3.cloned.1.call-update
  119.6 0.0 all-gather.5.cloned.1.call-start
  119.6 76.6 %all-reduce.3.cloned.1.call-done = f32[1,384,384]{2,1,0:T(8,128)} async-done(((f32[1,384,384]{2,1,0:T(8,128)}), f32[1,384,384]{2,1,0:T(8,128)}) %all-reduce.3.cloned.1.call-update) | async-done | bytes 589840 | tf_op jit(solution)/shard_map/psum | solution.py:35
  196.2 1.8 multiply_reduce_fusion.2
  198.0 6.3 %psum.44 = f32[]{:T(128)} all-reduce(f32[]{:T(128)} %multiply_reduce_fusion.2), channel_id=1, replica_groups=mesh['term'=8,'sector'=4] {'sector'}, use_global_device_ids=true, to_apply=%region_7.8 | all-reduce | flops 1 | bytes 8 | tf_op jit(solution)/shard_map/psum | solution.py:28
  204.9 1.9 multiply_reduce_fusion.1
  206.8 7.2 %psum.45 = f32[]{:T(128)} all-reduce(f32[]{:T(128)} %get-tuple-element.122), channel_id=1, replica_groups=mesh['term'=8,'sector'=4] {'sector'}, use_global_device_ids=true, to_apply=%region_9.10 | all-reduce | flops 1 | bytes 8 | tf_op jit(solution)/shard_map/psum | solution.py:28
  214.7 0.9 broadcast_multiply_fusion
  215.6 0.0 all-gather.5.cloned.1.call-update
  215.6 0.0 reduce-scatter.5.cloned.1.call-start
  215.7 22.5 %all-gather.5.cloned.1.call-done = f32[4,384,384]{2,1,0:T(8,128)} async-done(((f32[1,384,384]{2,1,0:T(8,128)}), f32[4,384,384]{2,1,0:T(8,128)}) %all-gather.5.cloned.1.call-update) | async-done | bytes 2359312 | tf_op jit(solution)/shard_map/all_gather | solution.py:32
  238.2 0.2 broadcast.6
  238.3 39.8 %while.21 = (s32[]{:T(128)}, f32[4,384,384]{2,1,0:T(8,128)S(1)}, s32[]{:T(128)}, s32[1,4]{1,0:T(1,128)S(1)}, f32[4,384,384]{2,1,0:T(8,128)}, /*index=5*/s32[1,4]...) while((s32[]{:T(128)}, f32[4,384,384]{2,1,0:T(8,128)S(1)}, ...), condition=%wide.region_11.12_spmd, body=%wide.region_10.11_spmd.sunk | while | flops 1359101952 | bytes 5308675 | solution.py:24
  239.0 0.6 constant_dynamic-slice_fusion.12
  243.2 2.5 fusion.46
  245.8 2.3 fusion.47
  248.8 0.6 constant_dynamic-slice_fusion.12
  253.0 2.5 fusion.46
  255.5 2.3 fusion.47
  258.6 0.6 constant_dynamic-slice_fusion.12
  262.8 2.5 fusion.46
  265.3 2.3 fusion.47
  268.3 0.6 constant_dynamic-slice_fusion.12
  272.5 2.5 fusion.46
  275.1 2.3 fusion.47
  278.1 1.4 copy-done
  279.5 0.0 reduce-scatter.5.cloned.1.call-update
  279.5 0.0 all-reduce.5.cloned.1.call-start
  279.6 32.9 %reduce-scatter.5.cloned.1.call-done = f32[1,384,384]{2,1,0:T(8,128)} async-done(((f32[4,384,384]{2,1,0:T(8,128)}), f32[1,384,384]{2,1,0:T(8,128)}) %reduce-scatter.5.cloned.1.call-update) | async-done | bytes 589840 | tf_op jit(solution)/shard_map/reduce_scatter | solution.py:34
  312.5 0.0 all-reduce.5.cloned.1.call-update
  312.5 76.5 %all-reduce.5.cloned.1.call-done = f32[1,384,384]{2,1,0:T(8,128)} async-done(((f32[1,384,384]{2,1,0:T(8,128)}), f32[1,384,384]{2,1,0:T(8,128)}) %all-reduce.5.cloned.1.call-update) | async-done | bytes 589840 | tf_op jit(solution)/shard_map/psum | solution.py:35
  389.0 1.8 multiply_reduce_fusion
  390.8 6.3 %psum.47 = f32[]{:T(128)} all-reduce(f32[]{:T(128)} %multiply_reduce_fusion), channel_id=1, replica_groups=mesh['term'=8,'sector'=4] {'sector'}, use_global_device_ids=true, to_apply=%region_15.16 | all-reduce | flops 1 | bytes 8 | tf_op jit(solution)/shard_map/psum | solution.py:28
  397.8 0.6 pad_maximum_fusion
  398.3 2.1 divide_subtract_fusion
  (14 shorter events, 0.4 us)
Async XLA Ops:
  7.2 38.2 %copy-start.4 = (s32[1,4]{1,0:T(1,128)S(1)}, s32[1,4]{1,0:T(1,128)}, u32[]{:S(2)}) copy-start(s32[1,4]{1,0:T(1,128)} %param.16) | copy-start | bytes 52
  7.2 38.2 %copy-start.5 = (s32[1,4]{1,0:T(1,128)S(1)}, s32[1,4]{1,0:T(1,128)}, u32[]{:S(2)}) copy-start(s32[1,4]{1,0:T(1,128)} %param.15) | copy-start | bytes 52
  7.2 38.0 %all-gather.3.cloned.1.call-start = ((), (), s32[]{:S(2)}) async-start(), calls=%async_computation.2 | async-start | bytes 2949120 | tf_op jit(solution)/shard_map/all_gather | solution.py:32
  20.7 98.9 %reduce-scatter.3.cloned.1.call-start = ((), (), s32[]{:S(2)}) async-start(), calls=%async_computation.3 | async-start | bytes 2949120 | tf_op jit(solution)/shard_map/reduce_scatter | solution.py:34
  85.1 1.4 copy-start.1
  85.1 111.0 %copy-start.2 = (f32[1,384,384]{2,1,0:T(8,128)S(1)}, f32[1,384,384]{2,1,0:T(8,128)}, u32[]{:S(2)}) copy-start(f32[1,384,384]{2,1,0:T(8,128)} %param.11) | copy-start | bytes 1769476
  85.2 119.8 %copy-start.3 = (f32[1,384,384]{2,1,0:T(8,128)S(1)}, f32[1,384,384]{2,1,0:T(8,128)}, u32[]{:S(2)}) copy-start(f32[1,384,384]{2,1,0:T(8,128)} %param.12) | copy-start | bytes 1769476
  86.6 109.6 %all-reduce.3.cloned.1.call-start = ((), (), s32[]{:S(2)}) async-start(), calls=%async_computation.4 | async-start | bytes 1179648 | tf_op jit(solution)/shard_map/psum | solution.py:35
  119.6 118.6 %all-gather.5.cloned.1.call-start = ((), (), s32[]{:S(2)}) async-start(), calls=%async_computation.5 | async-start | bytes 2949120 | tf_op jit(solution)/shard_map/all_gather | solution.py:32
  215.6 96.9 %reduce-scatter.5.cloned.1.call-start = ((), (), s32[]{:S(2)}) async-start(), calls=%async_computation.6 | async-start | bytes 2949120 | tf_op jit(solution)/shard_map/reduce_scatter | solution.py:34
  278.1 1.4 copy-start
  279.5 109.5 %all-reduce.5.cloned.1.call-start = ((), (), s32[]{:S(2)}) async-start(), calls=%async_computation.7 | async-start | bytes 1179648 | tf_op jit(solution)/shard_map/psum | solution.py:35
Sparse Core Ops, SparseCore 0:
  20.8 24.3 all-gather.2
  86.7 32.8 reduce-scatter.2
  122.9 73.2 all-reduce.2
  215.7 22.4 all-gather.4
  279.7 32.8 reduce-scatter.4
  315.7 73.2 all-reduce.4
where the time goes:
time: 409 us; the launch traced here: 407 us
  waiting for transfers between devices  266 us (65%)
  matrix products  38.7 us (9%)
  loops' own time  35.8 us (9%)
  blocking collectives  28.7 us (7%)
  between operations  16.9 us (4%)
  other arithmetic  12.8 us (3%)
  local copies, waits for them, and re-layouts  8.2 us (2%)
    psum x2, waiting for transfers between devices, sigma_blocks(): return lax.psum(owned_sum, 'term')  153 us
    reduce_scatter x2, waiting for transfers between devices, sigma_blocks(): lax.psum_scatter(partial_value, 'sector', scatter_dimension=0, tiled=True)  65.8 us
    all_gather x2, waiting for transfers between devices, sigma_blocks(): gathered = lax.all_gather(vector, 'sector', axis=0, tiled=True)  47 us
    another operation x2, loops' own time, apply_pairs(): lax.fori_loop(0, pair_count[0], one_pair, jnp.zeros(gathered.shape, jnp.f...  35.8 us
    psum x4, blocking collectives, global_sums(): return lax.psum((values[0],), 'sector')  28.7 us
    dot_general x8, matrix products, one_pair(): inner_prod = jnp.dot(left_block, source, precision=lax.Precision.HIGHEST)  20 us
    dot_general x8, matrix products, one_pair(): lax.dot_general(inner_prod, right_block, (((1,), (1,)), ((), ())), precis...  18.6 us
  transfers between devices with their start and end apart: 6, of which 6 were waited for; matrix products, arithmetic and copies ran while one was open for 0% of the time, Pallas kernels for 0%

commit v1 on v0

--- a/solution.py
+++ b/solution.py
@@ -29,7 +29,14 @@
 
 
 def sigma_blocks(vector, left_ops, right_ops, pair_in, pair_out, pair_count):
-    gathered = lax.all_gather(vector, "sector", axis=0, tiled=True)
+    ring = [vector]
+    for hop in range(3):
+        ring.append(lax.ppermute(ring[-1], "sector", [(dev, (dev + 1) % 4) for dev in range(4)]))
+    gathered = jnp.roll(
+        jnp.concatenate(ring[::-1], axis=0),
+        (lax.axis_index("sector") + 1) * ring[0].shape[0],
+        axis=0,
+    )
     partial_value = apply_pairs(gathered, left_ops, right_ops, pair_in, pair_out, pair_count)
     owned_sum = lax.psum_scatter(partial_value, "sector", scatter_dimension=0, tiled=True)
     return lax.psum(owned_sum, "term")

time: 409 us -> 420 us (1.027)
  waiting for transfers between devices: 266 us -> 273 us
    ppermute x0 -> x6, waiting for transfers between devices: none -> 55.8 us  [sigma_blocks(): lax.ppermute(ring[-1], 'sector', [(dev, (dev + 1) % 4) for dev in range(4)])]
    all_gather x2 -> x0, waiting for transfers between devices: 47 us -> none  [sigma_blocks(): gathered = lax.all_gather(vector, 'sector', axis=0, tiled=True)]
    concatenate x0 -> x2, other arithmetic: none -> 5.42 us  [sigma_blocks(): jnp.roll(jnp.concatenate(ring[::-1], axis=0), (lax.axis_index('sector') +...]
  transfers between devices with their start and end apart: 6 -> 10, of which waited for: 6 -> 10; matrix products, arithmetic and copies ran while one was open for 0% -> 0% of each run, Pallas kernels for 0% -> 0%
where the time goes in v1:
time: 420 us; the launch traced here: 419 us
  waiting for transfers between devices  273 us (65%)
  matrix products  38.7 us (9%)
  loops' own time  35.5 us (8%)
  blocking collectives  28.7 us (7%)
  other arithmetic  16.7 us (4%)
  between operations  16.5 us (4%)
  local copies, waits for them, and re-layouts  8.76 us (2%)
    psum x2, waiting for transfers between devices, sigma_blocks(): return lax.psum(owned_sum, 'term')  153 us
    reduce_scatter x2, waiting for transfers between devices, sigma_blocks(): lax.psum_scatter(partial_value, 'sector', scatter_dimension=0, tiled=True)  64.3 us
    ppermute x6, waiting for transfers between devices, sigma_blocks(): lax.ppermute(ring[-1], 'sector', [(dev, (dev + 1) % 4) for dev in range(4)])  55.8 us
    another operation x2, loops' own time, apply_pairs(): lax.fori_loop(0, pair_count[0], one_pair, jnp.zeros(gathered.shape, jnp.f...  35.5 us
    psum x4, blocking collectives, global_sums(): return lax.psum((values[0],), 'sector')  28.7 us
    dot_general x8, matrix products, one_pair(): inner_prod = jnp.dot(left_block, source, precision=lax.Precision.HIGHEST)  20.1 us
    dot_general x8, matrix products, one_pair(): lax.dot_general(inner_prod, right_block, (((1,), (1,)), ((), ())), precis...  18.6 us
  transfers between devices with their start and end apart: 10, of which 10 were waited for; matrix products, arithmetic and copies ran while one was open for 0% of the time, Pallas kernels for 0%

profile of v1, /device:TPU:0, one launch (start us, length us, event | category | flops | bytes accessed | tf_op | source)
XLA Modules:
  0.0 418.5 jit_solution(6998843743295864998)
XLA Ops:
  7.2 0.0 reduce-scatter.3.cloned.1.call-start
  7.2 1.8 multiply_reduce_fusion.3
  9.0 9.0 %psum.42 = f32[]{:T(128)} all-reduce(f32[]{:T(128)} %multiply_reduce_fusion.3), channel_id=1, replica_groups=mesh['term'=8,'sector'=4] {'sector'}, use_global_device_ids=true, to_apply=%region_1.0 | all-reduce | flops 1 | bytes 8 | tf_op jit(solution)/shard_map/psum | solution.py:28
  18.7 1.1 broadcast_multiply_fusion.1
  19.8 0.1 collective-permute-start
  19.9 9.3 %collective-permute-done = f32[1,384,384]{2,1,0:T(8,128)S(1)} collective-permute-done((f32[1,384,384]{2,1,0:T(8,128)S(1)}, f32[1,384,384]{2,1,0:T(8,128)S(1)}, u32[]{:S(2)}, u32[]{:S(2)}) %collective-permute-start) | collective-permute-done | bytes 589856 | tf_op jit(solution)/shard_map/ppermute | solution.py:34
  29.2 9.3 %collective-permute-done.1 = f32[1,384,384]{2,1,0:T(8,128)S(1)} collective-permute-done((f32[1,384,384]{2,1,0:T(8,128)S(1)}, f32[1,384,384]{2,1,0:T(8,128)S(1)}, u32[]{:S(2)}, u32[]{:S(2)}) %collective-permute-start.1) | collective-permute-done | bytes 589856 | tf_op jit(solution)/shard_map/ppermute | solution.py:34
  38.5 9.3 %collective-permute-done.2 = f32[1,384,384]{2,1,0:T(8,128)S(1)} collective-permute-done((f32[1,384,384]{2,1,0:T(8,128)S(1)}, f32[1,384,384]{2,1,0:T(8,128)S(1)}, u32[]{:S(2)}, u32[]{:S(2)}) %collective-permute-start.2) | collective-permute-done | bytes 589856 | tf_op jit(solution)/shard_map/ppermute | solution.py:34
  47.8 2.7 fusion.32
  50.5 0.2 broadcast.7.clone
  50.7 0.5 copy-done.4
  51.2 39.8 %while.20 = (s32[]{:T(128)}, f32[4,384,384]{2,1,0:T(8,128)S(1)}, s32[]{:T(128)}, s32[1,4]{1,0:T(1,128)S(1)}, f32[4,384,384]{2,1,0:T(8,128)}, /*index=5*/s32[1,4]...) while((s32[]{:T(128)}, f32[4,384,384]{2,1,0:T(8,128)S(1)}, ...), condition=%wide.region_3.5_spmd, body=%wide.region_2.4_spmd.sunk | while | flops 1359101952 | bytes 5308675 | solution.py:24
  51.9 0.6 constant_dynamic-slice_fusion.10
  56.1 2.5 fusion.54
  58.6 2.3 fusion.55
  61.6 0.6 constant_dynamic-slice_fusion.10
  65.8 2.5 fusion.54
  68.4 2.3 fusion.55
  71.4 0.6 constant_dynamic-slice_fusion.10
  75.6 2.5 fusion.54
  78.2 2.3 fusion.55
  81.2 0.6 constant_dynamic-slice_fusion.10
  85.4 2.5 fusion.54
  88.0 2.3 fusion.55
  91.0 1.4 copy-done.1
  92.4 0.0 reduce-scatter.3.cloned.1.call-update
  92.4 0.0 all-reduce.3.cloned.1.call-start
  92.5 33.2 %reduce-scatter.3.cloned.1.call-done = f32[1,384,384]{2,1,0:T(8,128)} async-done(((f32[4,384,384]{2,1,0:T(8,128)}), f32[1,384,384]{2,1,0:T(8,128)}) %reduce-scatter.3.cloned.1.call-update) | async-done | bytes 589840 | tf_op jit(solution)/shard_map/reduce_scatter | solution.py:41
  125.7 0.0 all-reduce.3.cloned.1.call-update
  125.7 0.0 reduce-scatter.5.cloned.1.call-start
  125.7 76.6 %all-reduce.3.cloned.1.call-done = f32[1,384,384]{2,1,0:T(8,128)} async-done(((f32[1,384,384]{2,1,0:T(8,128)}), f32[1,384,384]{2,1,0:T(8,128)}) %all-reduce.3.cloned.1.call-update) | async-done | bytes 589840 | tf_op jit(solution)/shard_map/psum | solution.py:42
  202.3 1.8 multiply_reduce_fusion.2
  204.2 6.3 %psum.44 = f32[]{:T(128)} all-reduce(f32[]{:T(128)} %multiply_reduce_fusion.2), channel_id=1, replica_groups=mesh['term'=8,'sector'=4] {'sector'}, use_global_device_ids=true, to_apply=%region_7.9 | all-reduce | flops 1 | bytes 8 | tf_op jit(solution)/shard_map/psum | solution.py:28
  211.1 2.1 multiply_reduce_fusion.1
  213.1 7.2 %psum.45 = f32[]{:T(128)} all-reduce(f32[]{:T(128)} %get-tuple-element.123), channel_id=1, replica_groups=mesh['term'=8,'sector'=4] {'sector'}, use_global_device_ids=true, to_apply=%region_9.11 | all-reduce | flops 1 | bytes 8 | tf_op jit(solution)/shard_map/psum | solution.py:28
  221.1 0.1 collective-permute-start.3
  221.2 9.3 %collective-permute-done.3 = f32[1,384,384]{2,1,0:T(8,128)S(1)} collective-permute-done((f32[1,384,384]{2,1,0:T(8,128)S(1)}, f32[1,384,384]{2,1,0:T(8,128)S(1)}, u32[]{:S(2)}, u32[]{:S(2)}) %collective-permute-start.3) | collective-permute-done | bytes 589856 | tf_op jit(solution)/shard_map/ppermute | solution.py:34
  230.4 9.3 %collective-permute-done.4 = f32[1,384,384]{2,1,0:T(8,128)S(1)} collective-permute-done((f32[1,384,384]{2,1,0:T(8,128)S(1)}, f32[1,384,384]{2,1,0:T(8,128)S(1)}, u32[]{:S(2)}, u32[]{:S(2)}) %collective-permute-start.4) | collective-permute-done | bytes 589856 | tf_op jit(solution)/shard_map/ppermute | solution.py:34
  239.8 9.3 %collective-permute-done.5 = f32[1,384,384]{2,1,0:T(8,128)S(1)} collective-permute-done((f32[1,384,384]{2,1,0:T(8,128)S(1)}, f32[1,384,384]{2,1,0:T(8,128)S(1)}, u32[]{:S(2)}, u32[]{:S(2)}) %collective-permute-start.5) | collective-permute-done | bytes 589856 | tf_op jit(solution)/shard_map/ppermute | solution.py:34
  249.1 2.7 fusion.25
  251.8 0.2 broadcast.7
  251.9 39.6 %while.21 = (s32[]{:T(128)}, f32[4,384,384]{2,1,0:T(8,128)S(1)}, s32[]{:T(128)}, s32[1,4]{1,0:T(1,128)S(1)}, f32[4,384,384]{2,1,0:T(8,128)}, /*index=5*/s32[1,4]...) while((s32[]{:T(128)}, f32[4,384,384]{2,1,0:T(8,128)S(1)}, ...), condition=%wide.region_11.13_spmd, body=%wide.region_10.12_spmd.sunk | while | flops 1359101952 | bytes 5308675 | solution.py:24
  252.6 0.6 constant_dynamic-slice_fusion.12
  256.8 2.5 fusion.60
  259.3 2.3 fusion.61
  262.3 0.6 constant_dynamic-slice_fusion.12
  266.5 2.5 fusion.60
  269.1 2.3 fusion.61
  272.1 0.6 constant_dynamic-slice_fusion.12
  276.2 2.5 fusion.60
  278.8 2.3 fusion.61
  281.8 0.6 constant_dynamic-slice_fusion.12
  285.9 2.5 fusion.60
  288.5 2.3 fusion.61
  291.5 1.4 copy-done
  292.9 0.0 reduce-scatter.5.cloned.1.call-update
  292.9 0.0 all-reduce.5.cloned.1.call-start
  293.0 31.1 %reduce-scatter.5.cloned.1.call-done = f32[1,384,384]{2,1,0:T(8,128)} async-done(((f32[4,384,384]{2,1,0:T(8,128)}), f32[1,384,384]{2,1,0:T(8,128)}) %reduce-scatter.5.cloned.1.call-update) | async-done | bytes 589840 | tf_op jit(solution)/shard_map/reduce_scatter | solution.py:41
  324.1 0.0 all-reduce.5.cloned.1.call-update
  324.1 76.5 %all-reduce.5.cloned.1.call-done = f32[1,384,384]{2,1,0:T(8,128)} async-done(((f32[1,384,384]{2,1,0:T(8,128)}), f32[1,384,384]{2,1,0:T(8,128)}) %all-reduce.5.cloned.1.call-update) | async-done | bytes 589840 | tf_op jit(solution)/shard_map/psum | solution.py:42
  400.6 1.8 multiply_reduce_fusion
  402.4 6.3 %psum.47 = f32[]{:T(128)} all-reduce(f32[]{:T(128)} %multiply_reduce_fusion), channel_id=1, replica_groups=mesh['term'=8,'sector'=4] {'sector'}, use_global_device_ids=true, to_apply=%region_15.17 | all-reduce | flops 1 | bytes 8 | tf_op jit(solution)/shard_map/psum | solution.py:28
  409.3 0.6 pad_maximum_fusion
  409.9 2.1 divide_subtract_fusion
  (22 shorter events, 0.5 us)
Async XLA Ops:
  7.2 118.5 %reduce-scatter.3.cloned.1.call-start = ((), (), s32[]{:S(2)}) async-start(), calls=%async_computation.2 | async-start | bytes 2949120 | tf_op jit(solution)/shard_map/reduce_scatter | solution.py:41
  19.8 9.4 %collective-permute-start = (f32[1,384,384]{2,1,0:T(8,128)S(1)}, f32[1,384,384]{2,1,0:T(8,128)S(1)}, u32[]{:S(2)}, u32[]{:S(2)}) collective-permute-start(f32[1,384,384]{2,1,0:T(8,128)S(1)} %broadcast_multiply_fusion.1), channel_id=1, source_target_pairs={{0,1},{1,2},{2,3},{3,0},{4,5},{5,6},{6,7},{7,4},{8,9},{9,10},{10,1... | collective-permute-start | bytes 1769480 | tf_op jit(solution)/shard_map/ppermute | solution.py:34
  29.2 9.3 %collective-permute-start.1 = (f32[1,384,384]{2,1,0:T(8,128)S(1)}, f32[1,384,384]{2,1,0:T(8,128)S(1)}, u32[]{:S(2)}, u32[]{:S(2)}) collective-permute-start(f32[1,384,384]{2,1,0:T(8,128)S(1)} %collective-permute-done), channel_id=1, source_target_pairs={{0,1},{1,2},{2,3},{3,0},{4,5},{5,6},{6,7},{7,4},{8,9},{9,10},{10,1... | collective-permute-start | bytes 1769480 | tf_op jit(solution)/shard_map/ppermute | solution.py:34
  38.5 9.3 %collective-permute-start.2 = (f32[1,384,384]{2,1,0:T(8,128)S(1)}, f32[1,384,384]{2,1,0:T(8,128)S(1)}, u32[]{:S(2)}, u32[]{:S(2)}) collective-permute-start(f32[1,384,384]{2,1,0:T(8,128)S(1)} %collective-permute-done.1), channel_id=1, source_target_pairs={{0,1},{1,2},{2,3},{3,0},{4,5},{5,6},{6,7},{7,4},{8,9},{9,10},{10,1... | collective-permute-start | bytes 1769480 | tf_op jit(solution)/shard_map/ppermute | solution.py:34
  50.5 0.7 copy-start.4
  50.5 0.7 copy-start.5
  91.0 1.4 copy-start.1
  91.0 111.4 %copy-start.2 = (f32[1,384,384]{2,1,0:T(8,128)S(1)}, f32[1,384,384]{2,1,0:T(8,128)}, u32[]{:S(2)}) copy-start(f32[1,384,384]{2,1,0:T(8,128)} %param.13) | copy-start | bytes 1769476
  92.4 109.9 %all-reduce.3.cloned.1.call-start = ((), (), s32[]{:S(2)}) async-start(), calls=%async_computation.3 | async-start | bytes 1179648 | tf_op jit(solution)/shard_map/psum | solution.py:42
  125.7 198.4 %reduce-scatter.5.cloned.1.call-start = ((), (), s32[]{:S(2)}) async-start(), calls=%async_computation.4 | async-start | bytes 2949120 | tf_op jit(solution)/shard_map/reduce_scatter | solution.py:41
  221.1 9.4 %collective-permute-start.3 = (f32[1,384,384]{2,1,0:T(8,128)S(1)}, f32[1,384,384]{2,1,0:T(8,128)S(1)}, u32[]{:S(2)}, u32[]{:S(2)}) collective-permute-start(f32[1,384,384]{2,1,0:T(8,128)S(1)} %broadcast_multiply_fusion), channel_id=1, source_target_pairs={{0,1},{1,2},{2,3},{3,0},{4,5},{5,6},{6,7},{7,4},{8,9},{9,10},{10,1... | collective-permute-start | bytes 1769480 | tf_op jit(solution)/shard_map/ppermute | solution.py:34
  230.4 9.3 %collective-permute-start.4 = (f32[1,384,384]{2,1,0:T(8,128)S(1)}, f32[1,384,384]{2,1,0:T(8,128)S(1)}, u32[]{:S(2)}, u32[]{:S(2)}) collective-permute-start(f32[1,384,384]{2,1,0:T(8,128)S(1)} %collective-permute-done.3), channel_id=1, source_target_pairs={{0,1},{1,2},{2,3},{3,0},{4,5},{5,6},{6,7},{7,4},{8,9},{9,10},{10,1... | collective-permute-start | bytes 1769480 | tf_op jit(solution)/shard_map/ppermute | solution.py:34
  239.8 9.3 %collective-permute-start.5 = (f32[1,384,384]{2,1,0:T(8,128)S(1)}, f32[1,384,384]{2,1,0:T(8,128)S(1)}, u32[]{:S(2)}, u32[]{:S(2)}) collective-permute-start(f32[1,384,384]{2,1,0:T(8,128)S(1)} %collective-permute-done.4), channel_id=1, source_target_pairs={{0,1},{1,2},{2,3},{3,0},{4,5},{5,6},{6,7},{7,4},{8,9},{9,10},{10,1... | collective-permute-start | bytes 1769480 | tf_op jit(solution)/shard_map/ppermute | solution.py:34
  291.5 1.4 copy-start
  291.5 118.4 %copy-start.3 = (f32[1,384,384]{2,1,0:T(8,128)S(1)}, f32[1,384,384]{2,1,0:T(8,128)}, u32[]{:S(2)}) copy-start(f32[1,384,384]{2,1,0:T(8,128)} %param.14) | copy-start | bytes 1769476
  292.9 107.7 %all-reduce.5.cloned.1.call-start = ((), (), s32[]{:S(2)}) async-start(), calls=%async_computation.5 | async-start | bytes 1179648 | tf_op jit(solution)/shard_map/psum | solution.py:42
Sparse Core Ops, SparseCore 0:
  92.5 33.0 reduce-scatter.2
  129.0 73.2 all-reduce.2
  293.1 31.0 reduce-scatter.4
  327.4 73.2 all-reduce.4
